TPU v7x, 512 devices: a whole 4x4x16 slice. The times are simulated.
512 devices in a mesh: dp: 32 (over y, x, core), tensor: 16 (over z).
Axes of the slice: x: 4, y: 4, z: 16, core: 2. Of those that a mesh axis runs over, the one named last changes fastest.
Arguments:
- tokens: bfloat16 [16384, 8192], P('dp', 'tensor'), may hold values from -6 to 6
- row_adapter_index: int32 [16384, 1], P('dp'), may hold values from 0 to 255; in each aligned block of 512 rows (0 to 511, 512 to 1023, ...) at most 4 rows name the same one
- adapter_storage_slot: int32 [256], replicated, may hold values from 0 to 255, each once
- key_value_base_weight: bfloat16 [8192, 2, 1024], P('tensor'), may hold values from -0.09375 to 0.09375
- adapter_down_weight: bfloat16 [256, 8192, 128], P('dp', 'tensor'), may hold values from -0.0625 to 0.0625
- adapter_up_weight: bfloat16 [256, 2, 64, 1024], P('dp', None, None, 'tensor'), may hold values from -0.75 to 0.75
Outputs:
- key_value: bfloat16 [16384, 2, 1024], P('dp', None, 'tensor')
Inputs may be any that keep to these rules, and one draw needn't show every extreme that they name: `row_adapter_index`: within the rows of one index of dp no adapter is named by more than 4 rows, a bound that some block reaches. `adapter_storage_slot`: A permutation of the slots.
All inputs are finite; a program needn't handle non-finite values.
Results may differ from a plain program's by a relative error of at most 0.0034.
Values may be sent and summed in bfloat16 or wider, within the bound.
A program may use at most 64 MiB of HBM per device.

v0:
```python
import jax
import jax.numpy as jnp
from jax import lax
from jax.sharding import PartitionSpec as P

adapter_scale = 0.5


def per_device(
    tokens,
    row_adapter_index,
    adapter_storage_slot,
    key_value_base_weight,
    adapter_down_weight,
    adapter_up_weight,
):
    row_count, shard_width = tokens.shape
    local_adapter_slots = adapter_down_weight.shape[0]
    groups = lax.axis_size("dp")
    experts = local_adapter_slots * groups
    capacity = max(2, 2 * row_count // experts)
    doubled_rank = adapter_down_weight.shape[2]
    adapter_of = row_adapter_index[:, 0]
    columns = lax.broadcasted_iota(jnp.int32, (row_count, experts), 1)
    onehot = (adapter_of[:, None] == columns).astype(jnp.int32)
    earlier = jnp.cumsum(onehot, axis=0) - onehot
    position = jnp.sum(earlier * onehot, axis=1)
    storage_device = jnp.sum(onehot * adapter_storage_slot[None, :], axis=1)
    target = storage_device * capacity + position
    outbox = jnp.zeros((experts * capacity, shard_width), tokens.dtype).at[target].set(tokens)
    outbox = outbox.reshape(groups, local_adapter_slots, capacity, shard_width)
    partials = jnp.einsum(
        "rd,djn->rjn", tokens, key_value_base_weight, preferred_element_type=jnp.float32
    )
    base = lax.psum_scatter(partials, "tensor", scatter_dimension=2, tiled=True)
    pieces_sum = jnp.einsum(
        "sekd,edr->sekr",
        lax.all_to_all(outbox, "dp", split_axis=0, concat_axis=0, tiled=True),
        adapter_down_weight,
        preferred_element_type=jnp.float32,
    )
    reduced_rows = lax.psum(pieces_sum, "tensor").astype(jnp.bfloat16)
    dims_now = reduced_rows.shape
    reduced_rows = reduced_rows.reshape(dims_now[0], dims_now[1], dims_now[2], 2, doubled_rank // 2)
    adapter_delta = jnp.einsum(
        "upgtl,ptlz->upgtz", reduced_rows, adapter_up_weight, preferred_element_type=jnp.float32
    )
    adapter_delta = (adapter_scale * adapter_delta).astype(jnp.bfloat16)
    returned = lax.all_to_all(adapter_delta, "dp", split_axis=0, concat_axis=0, tiled=True)
    returned_flat = returned.reshape(experts * capacity, 2, returned.shape[-1])
    update_rows = returned_flat[target]
    return (base + update_rows.astype(jnp.float32)).astype(jnp.bfloat16)


def solution(mesh):
    placed = (
        P("dp", "tensor"),
        P("dp", None),
        P(),
        P("tensor", None, None),
        P("dp", "tensor", None),
        P("dp", None, None, "tensor"),
    )
    return jax.shard_map(
        per_device, mesh=mesh, in_specs=placed, out_specs=P("dp", None, "tensor"), check_vma=False
    )
```

profile of v0, /device:TPU:1, one launch (start us, length us, event | category | flops | bytes accessed | tf_op | source)
XLA Modules:
  0.0 144.0 jit_solution(11326901580064575148)
XLA Ops:
  6.5 0.0 copy-start
  6.5 0.0 reduce-scatter.2.cloned.1.call-start
  6.5 1.6 %copy-done = bf16[512,2,1024]{2,1,0:T(2,128)(2,1)S(1)} copy-done((bf16[512,2,1024]{2,1,0:T(2,128)(2,1)S(1)}, bf16[512,2,1024]{2,1,0:T(2,128)(2,1)}, u32[]{:S(2)}) %copy-start) | copy-done | bytes 2097176
  8.1 4.3 %fusion = f32[512,2,1024]{0,2,1:T(8,128)} fusion(bf16[512,2,1024]{2,1,0:T(2,128)(2,1)S(1)} %copy-done, bf16[512,512]{1,0:T(8,128)(2,1)} %param.6), kind=kOutput, calls=%fused_computation.2 | convolution fusion | flops 1073741824 | bytes 6815744 | tf_op jit(solution)/shard_map/rd,djn->rjn/dot_general | solution.py:32
  12.4 0.0 copy-start.2
  12.4 0.0 reduce-scatter.2.cloned.1.call-update
  12.5 0.0 copy-start.3
  12.5 0.6 copy-done.2
  13.1 0.1 copy.19
  13.2 0.2 fusion.10
  13.5 0.1 copy.20
  13.6 0.0 copy-done.3
  13.7 0.4 select_reduce_fusion
  14.0 3.2 %scatter_custom_fusion = bf16[1024,512]{1,0:T(8,128)(2,1)S(1)} fusion(s32[512]{0:T(512)S(1)} %bitcast.51, bf16[512,512]{1,0:T(8,128)(2,1)} %param.6, bf16[]{:T(256)} %constant.5.clone.1), kind=kCustom, calls=%fused_computation.20 | custom fusion | bytes 1049088 | tf_op jit(solution)/shard_map/scatter | solution.py:30
  17.3 1.1 reshape.51
  18.4 0.0 copy-start.1
  18.4 27.9 %all_to_all.10 = bf16[32,8,4,512]{3,2,1,0:T(4,128)(2,1)S(1)} all-to-all(bf16[32,8,4,512]{3,2,1,0:T(4,128)(2,1)} %reshape.51), channel_id=1, replica_groups=mesh['dp'=32,'tensor'=16] {'dp'}, dimensions={0} | all-to-all | bytes 2097152 | tf_op jit(solution)/shard_map/all_to_all | solution.py:38
  46.3 0.0 copy-done.1
  46.3 0.0 copy-start.4
  46.3 0.8 convolution_bitcast_fusion
  47.1 61.2 %all-reduce.1 = bf16[32,8,4,128]{3,0,2,1:T(8,128)(2,1)S(1)} all-reduce(f32[32,8,4,128]{3,0,2,1:T(8,128)S(1)} %convolution_bitcast_fusion), channel_id=1, replica_groups=mesh['dp'=32,'tensor'=16] {'tensor'}, use_global_device_ids=true, to_apply=%region_6.7 | all-reduce | flops 131072 | bytes 786432 | tf_op jit(solution)/shard_map/psum | solution.py:42
  108.3 0.2 reshape.52
  108.5 0.0 copy-done.4
  108.5 0.3 fusion.3
  108.8 0.3 copy.36
  109.1 1.1 reshape.75
  110.2 13.0 %all-to-all-start.1 = ((bf16[32,2,2048]{2,1,0:T(2,128)(2,1)}), bf16[32,2,2048]{2,1,0:T(2,128)(2,1)S(1)}, u32[]{:S(2)}, u32[]{:S(2)}) async-start(bf16[32,2,2048]{2,1,0:T(2,128)(2,1)} %reshape.75), calls=%async_computation.2 | async-start | bytes 524288 | tf_op jit(solution)/shard_map/all_to_all | solution.py:49
  123.3 8.9 %all-to-all-done.1 = bf16[32,2,2048]{2,1,0:T(2,128)(2,1)S(1)} async-done(((bf16[32,2,2048]{2,1,0:T(2,128)(2,1)}), bf16[32,2,2048]{2,1,0:T(2,128)(2,1)S(1)}, u32[]{:S(2)}, u32[]{:S(2)}) %all-to-all-start.1) | async-done | bytes 262176 | tf_op jit(solution)/shard_map/all_to_all | solution.py:49
  132.1 0.4 reshape.76
  132.5 0.2 copy.24
  132.7 0.5 copy.25
  133.2 2.1 %gather_fusion = bf16[512,2,64]{2,1,0:T(2,128)(2,1)S(1)} fusion(bf16[1024,2,64]{2,1,0:T(2,128)(2,1)S(1)} %copy.25, s32[1024]{0:T(1024)S(1)} %pad_clamp_fusion), kind=kCustom, calls=%fused_computation | custom fusion | bytes 264192 | tf_op jit(solution)/shard_map/gather | solution.py:51
  135.4 0.1 copy.26
  135.5 0.0 reduce-scatter.2.cloned.1.call-done
  135.5 1.6 %add_convert_fusion = bf16[512,2,64]{0,2,1:T(8,128)(2,1)} fusion(f32[512,2,64]{0,2,1:T(8,128)} %reduce-scatter.2.cloned.1.call-done, bf16[512,2,64]{0,2,1:T(8,128)(2,1)S(1)} %copy.26), kind=kLoop, calls=%fused_computation.23 | loop fusion | flops 196608 | bytes 524288 | tf_op jit(solution)/shard_map/convert_element_type | solution.py:52
  (8 shorter events, 0.1 us)
Async XLA Ops:
  6.5 1.6 %copy-start = (bf16[512,2,1024]{2,1,0:T(2,128)(2,1)S(1)}, bf16[512,2,1024]{2,1,0:T(2,128)(2,1)}, u32[]{:S(2)}) copy-start(bf16[512,2,1024]{2,1,0:T(2,128)(2,1)} %param.9) | copy-start | bytes 6291460
  6.5 129.0 %reduce-scatter.2.cloned.1.call-start = ((), (), s32[]{:S(2)}) async-start(), calls=%async_computation.3 | async-start | bytes 4456448 | tf_op jit(solution)/shard_map/reduce_scatter | solution.py:35
  12.4 0.7 copy-start.2
  12.5 1.2 copy-start.3
  18.4 27.9 %copy-start.1 = (bf16[8,512,128]{2,1,0:T(8,128)(2,1)S(1)}, bf16[8,512,128]{2,1,0:T(8,128)(2,1)}, u32[]{:S(2)}) copy-start(bf16[8,512,128]{2,1,0:T(8,128)(2,1)} %param.10) | copy-start | bytes 3145732
  46.3 62.3 %copy-start.4 = (bf16[8,2,64,64]{3,2,1,0:T(8,128)(2,1)S(1)}, bf16[8,2,64,64]{3,2,1,0:T(8,128)(2,1)}, u32[]{:S(2)}) copy-start(bf16[8,2,64,64]{3,2,1,0:T(8,128)(2,1)} %param.11) | copy-start | bytes 393220
  110.2 22.0 %all-to-all-start.1 = ((bf16[32,2,2048]{2,1,0:T(2,128)(2,1)}), bf16[32,2,2048]{2,1,0:T(2,128)(2,1)S(1)}, u32[]{:S(2)}, u32[]{:S(2)}) async-start(bf16[32,2,2048]{2,1,0:T(2,128)(2,1)} %reshape.75), calls=%async_computation.2 | async-start | bytes 524288 | tf_op jit(solution)/shard_map/all_to_all | solution.py:49
Sparse Core Ops, SparseCore 0:
  12.6 79.6 reduce-scatter.1
where the time goes:
time: 144 us
  blocking collectives  89.1 us (62%)
  between operations  13.6 us (9%)
  starting transfers between devices  13 us (9%)
  local copies, waits for them, and re-layouts  11.8 us (8%)
  waiting for transfers between devices  8.92 us (6%)
  matrix products  5.38 us (4%)
  other arithmetic  2.28 us (2%)
    psum x1, blocking collectives, per_device(): reduced_rows = lax.psum(pieces_sum, 'tensor').astype(jnp.bfloat16)  61.2 us
    all_to_all x1, blocking collectives, per_device(): lax.all_to_all(outbox, 'dp', split_axis=0, concat_axis=0, tiled=True)  27.9 us
    all_to_all x1, starting transfers between devices, per_device(): lax.all_to_all(adapter_delta, 'dp', split_axis=0, concat_axis=0, tiled=True)  13 us
    all_to_all x1, waiting for transfers between devices, per_device(): lax.all_to_all(adapter_delta, 'dp', split_axis=0, concat_axis=0, tiled=True)  8.89 us
    dot_general x1, matrix products, per_device(): jnp.einsum('rd,djn->rjn', tokens, key_value_base_weight, preferred_elemen...  4.31 us
    unnamed x13, local copies, waits for them, and re-layouts  3.69 us
    scatter x1, local copies, waits for them, and re-layouts, per_device(): jnp.zeros((experts * capacity, shard_width), tokens.dtype).at[target]  3.22 us
  transfers between devices with their start and end apart: 2, of which 1 were waited for; matrix products, arithmetic and copies ran while one was open for 8% of the time, Pallas kernels for 0%

commit v1 on v0

--- a/solution.py
+++ b/solution.py
@@ -39,7 +39,7 @@
         adapter_down_weight,
         preferred_element_type=jnp.float32,
     )
-    reduced_rows = lax.psum(pieces_sum, "tensor").astype(jnp.bfloat16)
+    reduced_rows = jnp.sum(lax.all_gather(pieces_sum, "tensor"), axis=0).astype(jnp.bfloat16)
     dims_now = reduced_rows.shape
     reduced_rows = reduced_rows.reshape(dims_now[0], dims_now[1], dims_now[2], 2, doubled_rank // 2)
     adapter_delta = jnp.einsum(

time: 144 us -> 236 us (1.64)
  the two profiles are of different devices: /device:TPU:1 before, /device:TPU:4 now
where the time goes in v1:
time: 236 us; the launch traced here: 235 us
  waiting for transfers between devices  167 us (71%)
  blocking collectives  25 us (11%)
  between operations  13.6 us (6%)
  local copies, waits for them, and re-layouts  10.4 us (4%)
  starting transfers between devices  7.45 us (3%)
  other arithmetic  6.77 us (3%)
  matrix products  5.22 us (2%)
    all_gather x1, waiting for transfers between devices, per_device(): lax.all_gather(pieces_sum, 'tensor')  103 us
    reduce_scatter x1, waiting for transfers between devices, per_device(): base = lax.psum_scatter(partials, 'tensor', scatter_dimension=2, tiled=True)  56.8 us
    all_to_all x1, blocking collectives, per_device(): lax.all_to_all(outbox, 'dp', split_axis=0, concat_axis=0, tiled=True)  25 us
    all_to_all x1, starting transfers between devices, per_device(): lax.all_to_all(adapter_delta, 'dp', split_axis=0, concat_axis=0, tiled=True)  7.41 us
    all_to_all x1, waiting for transfers between devices, per_device(): lax.all_to_all(adapter_delta, 'dp', split_axis=0, concat_axis=0, tiled=True)  6.75 us
  transfers between devices with their start and end apart: 3, of which 3 were waited for; matrix products, arithmetic and copies ran while one was open for 6% of the time, Pallas kernels for 0%

profile of v1, /device:TPU:4, one launch (start us, length us, event | category | flops | bytes accessed | tf_op | source)
XLA Modules:
  0.0 235.2 jit_solution(1538117031680890654)
XLA Ops:
  6.5 0.0 copy-start
  6.5 0.0 copy-start.3
  6.5 0.0 copy-start.4
  6.5 0.0 all-gather.3.cloned.1.call-start
  6.5 0.9 copy.18
  7.5 0.2 fusion.10
  7.8 0.1 copy.19
  7.9 0.0 copy-done.3
  7.9 0.0 copy-done.4
  7.9 0.4 select_reduce_fusion
  8.3 3.2 %scatter_custom_fusion = bf16[1024,512]{1,0:T(8,128)(2,1)S(1)} fusion(s32[512]{0:T(512)S(1)} %bitcast.53, bf16[512,512]{1,0:T(8,128)(2,1)} %param.6, bf16[]{:T(256)} %constant.6.clone.1), kind=kCustom, calls=%fused_computation.20 | custom fusion | bytes 1049088 | tf_op jit(solution)/shard_map/scatter | solution.py:30
  11.5 1.1 reshape.51
  12.7 0.0 copy-start.1
  12.7 25.0 %all_to_all.10 = bf16[32,8,4,512]{3,2,1,0:T(4,128)(2,1)S(1)} all-to-all(bf16[32,8,4,512]{3,2,1,0:T(4,128)(2,1)} %reshape.51), channel_id=1, replica_groups=mesh['dp'=32,'tensor'=16] {'dp'}, dimensions={0} | all-to-all | bytes 2097152 | tf_op jit(solution)/shard_map/all_to_all | solution.py:38
  37.6 0.0 copy-done.1
  37.7 0.0 copy-start.2
  37.7 1.6 convolution_bitcast_fusion
  39.3 0.0 all-gather.3.cloned.1.call-update
  39.3 0.0 reduce-scatter.2.cloned.1.call-start
  39.4 0.0 copy-done
  39.4 0.0 copy-done.2
  39.4 3.3 %fusion = f32[512,2,1024]{0,2,1:T(8,128)} fusion(bf16[512,2,1024]{2,1,0:T(2,128)(2,1)S(1)} %copy-done, bf16[512,512]{1,0:T(8,128)(2,1)S(1)} %copy-done.2), kind=kOutput, calls=%fused_computation.2 | convolution fusion | flops 1073741824 | bytes 6815744 | tf_op jit(solution)/shard_map/rd,djn->rjn/dot_general | solution.py:32
  42.7 0.0 reduce-scatter.2.cloned.1.call-update
  42.7 103.2 %all-gather.3.cloned.1.call-done = f32[512,8,4,128]{3,0,2,1:T(8,128)} async-done(((f32[32,8,4,128]{3,0,2,1:T(8,128)}), f32[512,8,4,128]{3,0,2,1:T(8,128)}) %all-gather.3.cloned.1.call-update) | async-done | bytes 8388624 | tf_op jit(solution)/shard_map/all_gather | solution.py:42
  145.9 0.0 copy-start.5
  145.9 4.5 %reduce_sum.29 = bf16[32,8,4,128]{3,0,2,1:T(8,128)(2,1)S(1)} reduce(f32[16,32,8,4,128]{4,1,0,3,2:T(8,128)} %bitcast.44, f32[]{:T(128)} %constant.16.clone.1), dimensions={0}, to_apply=%region_6.7 | reduce | flops 1966080 | bytes 8650756 | tf_op jit(solution)/shard_map/reduce_sum | solution.py:42
  150.4 0.2 reshape.73
  150.7 0.0 copy-done.5
  150.7 0.3 fusion.3
  151.0 0.3 copy.38
  151.2 1.1 reshape.76
  152.3 7.4 %all-to-all-start.1 = ((bf16[32,2,2048]{2,1,0:T(2,128)(2,1)}), bf16[32,2,2048]{2,1,0:T(2,128)(2,1)S(1)}, u32[]{:S(2)}, u32[]{:S(2)}) async-start(bf16[32,2,2048]{2,1,0:T(2,128)(2,1)} %reshape.76), calls=%async_computation.2 | async-start | bytes 524288 | tf_op jit(solution)/shard_map/all_to_all | solution.py:49
  159.8 6.7 %all-to-all-done.1 = bf16[32,2,2048]{2,1,0:T(2,128)(2,1)S(1)} async-done(((bf16[32,2,2048]{2,1,0:T(2,128)(2,1)}), bf16[32,2,2048]{2,1,0:T(2,128)(2,1)S(1)}, u32[]{:S(2)}, u32[]{:S(2)}) %all-to-all-start.1) | async-done | bytes 262176 | tf_op jit(solution)/shard_map/all_to_all | solution.py:49
  166.5 0.4 reshape.77
  166.9 0.2 copy.24
  167.1 0.5 copy.25
  167.6 2.1 gather_fusion
  169.7 0.1 copy.26
  169.9 56.8 %reduce-scatter.2.cloned.1.call-done = f32[512,2,64]{0,2,1:T(8,128)} async-done(((f32[512,2,1024]{0,2,1:T(8,128)}), f32[512,2,64]{0,2,1:T(8,128)}) %reduce-scatter.2.cloned.1.call-update) | async-done | bytes 262160 | tf_op jit(solution)/shard_map/reduce_scatter | solution.py:35
  226.7 1.6 add_convert_fusion
  (8 shorter events, 0.1 us)
Async XLA Ops:
  6.5 32.8 %copy-start = (bf16[512,2,1024]{2,1,0:T(2,128)(2,1)S(1)}, bf16[512,2,1024]{2,1,0:T(2,128)(2,1)}, u32[]{:S(2)}) copy-start(bf16[512,2,1024]{2,1,0:T(2,128)(2,1)} %param.9) | copy-start | bytes 6291460
  6.5 1.4 copy-start.3
  6.5 1.4 copy-start.4
  6.5 139.4 %all-gather.3.cloned.1.call-start = ((), (), s32[]{:S(2)}) async-start(), calls=%async_computation.4 | async-start | bytes 8912896 | tf_op jit(solution)/shard_map/all_gather | solution.py:42
  12.7 25.0 %copy-start.1 = (bf16[8,512,128]{2,1,0:T(8,128)(2,1)S(1)}, bf16[8,512,128]{2,1,0:T(8,128)(2,1)}, u32[]{:S(2)}) copy-start(bf16[8,512,128]{2,1,0:T(8,128)(2,1)} %param.10) | copy-start | bytes 3145732
  37.7 1.7 copy-start.2
  39.3 187.4 %reduce-scatter.2.cloned.1.call-start = ((), (), s32[]{:S(2)}) async-start(), calls=%async_computation.3 | async-start | bytes 4456448 | tf_op jit(solution)/shard_map/reduce_scatter | solution.py:35
  145.9 4.7 %copy-start.5 = (bf16[8,2,64,64]{3,2,1,0:T(8,128)(2,1)S(1)}, bf16[8,2,64,64]{3,2,1,0:T(8,128)(2,1)}, u32[]{:S(2)}) copy-start(bf16[8,2,64,64]{3,2,1,0:T(8,128)(2,1)} %param.11) | copy-start | bytes 393220
  152.3 14.2 %all-to-all-start.1 = ((bf16[32,2,2048]{2,1,0:T(2,128)(2,1)}), bf16[32,2,2048]{2,1,0:T(2,128)(2,1)S(1)}, u32[]{:S(2)}, u32[]{:S(2)}) async-start(bf16[32,2,2048]{2,1,0:T(2,128)(2,1)} %reshape.76), calls=%async_computation.2 | async-start | bytes 524288 | tf_op jit(solution)/shard_map/all_to_all | solution.py:49
Sparse Core Ops, SparseCore 0:
  39.4 106.4 all-gather.2
  148.8 77.9 reduce-scatter.1
